TPU v7x, 128 devices: a whole 4x4x4 slice. The times are simulated.
128 devices in a mesh: atom: 32 (over z, y, core), dp: 4 (over x).
Axes of the slice: x: 4, y: 4, z: 4, core: 2. Of those that a mesh axis runs over, the one named last changes fastest.
Arguments:
- activations: bfloat16 [512, 8192], P('dp'), may hold values from -6 to 6
- dictionary: bfloat16 [8192, 65536], P('dp', 'atom'), may hold values from -0.03535534 to 0.03535534
Outputs:
- sparse_codes: float32 [512, 65536], P('dp', 'atom')
- residual: float32 [512, 8192], P('atom', 'dp')
- new_dictionary: bfloat16 [8192, 65536], P('dp', 'atom')
All inputs are finite; a program needn't handle non-finite values.
Results may differ from a plain program's by a relative error of at most 0.0025.
Values may be sent and summed in bfloat16 or wider, within the bound.
No kernel may reach another device: no remote copies, remote signals or barrier semaphores. Data moves between devices by JAX's collectives and lax.ppermute only.
A program may use at most 128 MiB of HBM per device.

v0:
```python
import jax
import jax.numpy as jnp
from jax import lax
from jax.sharding import PartitionSpec as P

D = 8192
ITERS = 2
threshold = 0.05
step_size = 2.0
learn_rate = 1.0 / 16384.0
epsilon = 1e-12


def shrink(values):
    return values - jnp.clip(values, -threshold, threshold)


def product(left, right):
    return jnp.dot(
        left.astype(jnp.float32),
        right,
        precision=lax.Precision.HIGHEST,
        preferred_element_type=jnp.float32,
    )


def body(activations, dictionary):
    row_count = activations.shape[0]
    dict_wide = dictionary.astype(jnp.float32)
    feature_block = lax.all_to_all(activations, "dp", split_axis=1, concat_axis=0, tiled=True)
    inputs = feature_block.astype(jnp.float32)
    share_rows = feature_block.shape[0] // lax.axis_size("atom")
    offset = lax.axis_index("atom") * share_rows

    def residual_of(coded_rows):
        recon_part = product(coded_rows, dict_wide.T)
        summed = lax.psum(recon_part, "atom")
        full_residual = inputs - summed
        rounded = full_residual.astype(jnp.bfloat16)
        own_residual = lax.dynamic_slice_in_dim(full_residual, offset, share_rows, 0)
        return (rounded, own_residual)

    sparse_codes = jnp.zeros((row_count, dictionary.shape[1]), jnp.float32)
    rounded = feature_block
    coded_rows = None
    residual = None
    for iteration in range(ITERS):
        if iteration > 0:
            rounded, residual = residual_of(coded_rows)

        def encode_rows(first_row, row_total, source=rounded):
            return product(source, dict_wide)

        drive_term = lax.psum_scatter(
            encode_rows(jnp.int32(0), lax.axis_size("dp") * row_count),
            "dp",
            scatter_dimension=0,
            tiled=True,
        )
        sparse_codes = shrink(sparse_codes + step_size * drive_term)
        coded_rows = lax.all_gather(sparse_codes.astype(jnp.bfloat16), "dp", axis=0, tiled=True)
    rounded, residual = residual_of(coded_rows)
    gradient = product(rounded.T, coded_rows.astype(jnp.float32))
    updated = dict_wide + learn_rate * gradient
    squares = lax.psum(jnp.sum(updated * updated, axis=0), "dp")
    new_dictionary = (updated * lax.rsqrt(squares / D + epsilon)).astype(jnp.bfloat16)
    return (sparse_codes, residual, new_dictionary)


def solution(mesh):
    placed = (P("dp", None), P("dp", "atom"))
    return jax.shard_map(
        body,
        mesh=mesh,
        in_specs=placed,
        out_specs=(P("dp", "atom"), P("atom", "dp"), P("dp", "atom")),
        check_vma=False,
    )
```

profile of v0, /device:TPU:24, one launch (start us, length us, event | category | flops | bytes accessed | tf_op | source)
XLA Modules:
  0.0 507.2 jit_solution(12741930514416772770)
XLA Ops:
  7.2 0.0 reduce-scatter.3.cloned.1.call-start
  7.2 0.0 copy-start
  7.2 1.9 copy.8
  9.1 30.7 %all_to_all.19 = bf16[128,4,2048]{2,0,1:T(8,128)(2,1)S(1)} all-to-all(bf16[128,4,2048]{2,0,1:T(8,128)(2,1)S(1)} %bitcast.18), channel_id=1, replica_groups=mesh['atom'=32,'dp'=4] {'dp'}, dimensions={1} | all-to-all | bytes 4194304 | tf_op jit(solution)/shard_map/all_to_all | solution.py:30
  39.8 0.0 copy-done
  39.8 6.0 %fusion.7 = f32[512,2048]{1,0:T(8,128)} fusion(bf16[512,2048]{1,0:T(8,128)(2,1)S(1)} %bitcast.16, bf16[2048,2048]{1,0:T(8,128)(2,1)S(1)} %copy-done), kind=kOutput, calls=%fused_computation.16 | convolution fusion | flops 4294967296 | bytes 14680064 | tf_op jit(solution)/shard_map/dot_general | solution.py:19
  45.8 0.0 reduce-scatter.3.cloned.1.call-update
  45.8 0.0 all-gather.3.cloned.1.call-start
  45.9 47.2 %reduce-scatter.3.cloned.1.call-done = f32[128,2048]{1,0:T(8,128)} async-done(((f32[512,2048]{1,0:T(8,128)}), f32[128,2048]{1,0:T(8,128)}) %reduce-scatter.3.cloned.1.call-update) | async-done | bytes 1048592 | tf_op jit(solution)/shard_map/reduce_scatter | solution.py:54
  93.0 2.2 fusion.5
  95.2 0.0 all-gather.3.cloned.1.call-update
  95.2 0.0 all-reduce.3.cloned.1.call-start
  95.3 30.6 %all-gather.3.cloned.1.call-done = bf16[512,2048]{1,0:T(8,128)(2,1)} async-done(((bf16[128,2048]{1,0:T(8,128)(2,1)}), bf16[512,2048]{1,0:T(8,128)(2,1)}) %all-gather.3.cloned.1.call-update) | async-done | bytes 2097168 | tf_op jit(solution)/shard_map/all_gather | solution.py:61
  125.8 10.6 %fusion.8 = f32[512,2048]{1,0:T(8,128)} fusion(bf16[512,2048]{1,0:T(8,128)(2,1)} %all-gather.3.cloned.1.call-done, bf16[2048,2048]{1,0:T(8,128)(2,1)} %param.3), kind=kOutput, calls=%fused_computation.17 | convolution fusion | flops 4294967296 | bytes 14680064 | tf_op jit(solution)/shard_map/dot_general | solution.py:19
  136.4 0.0 all-reduce.3.cloned.1.call-update
  136.4 0.0 reduce-scatter.5.cloned.1.call-start
  136.5 112.7 %all-reduce.3.cloned.1.call-done = f32[512,2048]{1,0:T(8,128)} async-done(((f32[512,2048]{1,0:T(8,128)}), f32[512,2048]{1,0:T(8,128)}) %all-reduce.3.cloned.1.call-update) | async-done | bytes 4194320 | tf_op jit(solution)/shard_map/psum | solution.py:37
  249.2 11.2 %fusion.1 = f32[512,2048]{1,0:T(8,128)} fusion(bf16[2048,2048]{1,0:T(8,128)(2,1)} %param.3, f32[512,2048]{1,0:T(8,128)} %all-reduce.3.cloned.1.call-done, bf16[512,2048]{1,0:T(8,128)(2,1)S(1)} %bitcast.17), kind=kOutput, calls=%fused_computation.6 | convolution fusion | flops 4298113024 | bytes 18874368 | tf_op jit(solution)/shard_map/dot_general | solution.py:19
  260.4 0.0 copy-start.1
  260.4 0.0 reduce-scatter.5.cloned.1.call-update
  260.4 0.0 all-gather.5.cloned.1.call-start
  260.4 45.7 %reduce-scatter.5.cloned.1.call-done = f32[128,2048]{1,0:T(8,128)} async-done(((f32[512,2048]{1,0:T(8,128)}), f32[128,2048]{1,0:T(8,128)}) %reduce-scatter.5.cloned.1.call-update) | async-done | bytes 1048592 | tf_op jit(solution)/shard_map/reduce_scatter | solution.py:54
  306.1 0.0 copy-done.1
  306.1 2.6 fusion.6
  308.8 0.0 all-gather.5.cloned.1.call-update
  308.8 0.2 all-reduce.5.cloned.1.call-start
  309.0 30.4 %all-gather.5.cloned.1.call-done = bf16[512,2048]{1,0:T(8,128)(2,1)} async-done(((bf16[128,2048]{1,0:T(8,128)(2,1)}), bf16[512,2048]{1,0:T(8,128)(2,1)}) %all-gather.5.cloned.1.call-update) | async-done | bytes 2097168 | tf_op jit(solution)/shard_map/all_gather | solution.py:61
  339.4 10.6 %fusion.9 = f32[512,2048]{1,0:T(8,128)} fusion(bf16[512,2048]{1,0:T(8,128)(2,1)} %all-gather.5.cloned.1.call-done, bf16[2048,2048]{1,0:T(8,128)(2,1)} %param.3), kind=kOutput, calls=%fused_computation.18 | convolution fusion | flops 4294967296 | bytes 14680064 | tf_op jit(solution)/shard_map/dot_general | solution.py:19
  350.0 0.0 all-reduce.5.cloned.1.call-update
  350.0 112.7 %all-reduce.5.cloned.1.call-done = f32[512,2048]{1,0:T(8,128)} async-done(((f32[512,2048]{1,0:T(8,128)}), f32[512,2048]{1,0:T(8,128)}) %all-reduce.5.cloned.1.call-update) | async-done | bytes 4194320 | tf_op jit(solution)/shard_map/psum | solution.py:37
  462.7 0.0 copy-start.2
  462.7 2.9 convert_subtract_fusion
  465.7 0.7 constant_dynamic-slice_fusion
  466.3 0.0 copy-done.2
  466.3 11.3 %multiply_reduce_fusion = (f32[2048]{0:T(1024)S(1)}, f32[2048,2048]{1,0:T(8,128)}) fusion(bf16[2048,2048]{1,0:T(8,128)(2,1)} %param.3, bf16[512,2048]{1,0:T(8,128)(2,1)S(1)} %copy-done.2, f32[512,2048]{1,0:T(8,128)S(1)} %convert_subtract_fusion), kind=kOutput, calls=%fused_computation.1 | convolution fusion | flops 4316985344 | bytes 31465472 | tf_op jit(solution)/shard_map/dot_general | solution.py:19
  477.7 10.5 %psum.23 = f32[2048]{0:T(1024)S(1)} all-reduce(f32[2048]{0:T(1024)S(1)} %get-tuple-element.5), channel_id=1, replica_groups=mesh['atom'=32,'dp'=4] {'dp'}, use_global_device_ids=true, to_apply=%region_5.6 | all-reduce | flops 2048 | bytes 16384 | tf_op jit(solution)/shard_map/psum | solution.py:65
  488.2 12.1 %multiply_convert_fusion = bf16[2048,2048]{1,0:T(8,128)(2,1)} fusion(f32[2048,2048]{1,0:T(8,128)} %get-tuple-element.6, bf16[2048,2048]{1,0:T(8,128)(2,1)} %param.3, f32[2048]{0:T(1024)S(1)} %add_rsqrt_fusion), kind=kLoop, calls=%fused_computation | loop fusion | flops 20971520 | bytes 33562624 | tf_op jit(solution)/shard_map/convert_element_type | solution.py:66
  (1 shorter events, 0.0 us)
Async XLA Ops:
  7.2 85.9 %reduce-scatter.3.cloned.1.call-start = ((), (), s32[]{:S(2)}) async-start(), calls=%async_computation.3 | async-start | bytes 5242880 | tf_op jit(solution)/shard_map/reduce_scatter | solution.py:54
  7.2 32.6 %copy-start = (bf16[2048,2048]{1,0:T(8,128)(2,1)S(1)}, bf16[2048,2048]{1,0:T(8,128)(2,1)}, u32[]{:S(2)}) copy-start(bf16[2048,2048]{1,0:T(8,128)(2,1)} %param.3) | copy-start | bytes 25165828
  45.8 80.0 %all-gather.3.cloned.1.call-start = ((), (), s32[]{:S(2)}) async-start(), calls=%async_computation.4 | async-start | bytes 2621440 | tf_op jit(solution)/shard_map/all_gather | solution.py:61
  95.2 154.0 %all-reduce.3.cloned.1.call-start = ((), (), s32[]{:S(2)}) async-start(), calls=%async_computation.5 | async-start | bytes 8388608 | tf_op jit(solution)/shard_map/psum | solution.py:37
  136.4 169.7 %reduce-scatter.5.cloned.1.call-start = ((), (), s32[]{:S(2)}) async-start(), calls=%async_computation.6 | async-start | bytes 5242880 | tf_op jit(solution)/shard_map/reduce_scatter | solution.py:54
  260.4 45.8 %copy-start.1 = (f32[128,2048]{1,0:T(8,128)S(1)}, f32[128,2048]{1,0:T(8,128)}, u32[]{:S(2)}) copy-start(f32[128,2048]{1,0:T(8,128)} %reduce-scatter.3.cloned.1.call-done) | copy-start | bytes 3145732
  260.4 79.0 %all-gather.5.cloned.1.call-start = ((), (), s32[]{:S(2)}) async-start(), calls=%async_computation.7 | async-start | bytes 2621440 | tf_op jit(solution)/shard_map/all_gather | solution.py:61
  308.8 153.9 %all-reduce.5.cloned.1.call-start = ((), (), s32[]{:S(2)}) async-start(), calls=%async_computation.8 | async-start | bytes 8388608 | tf_op jit(solution)/shard_map/psum | solution.py:37
  462.7 3.6 copy-start.2
Sparse Core Ops, SparseCore 0:
  45.9 47.0 reduce-scatter.2
  95.3 30.4 all-gather.2
  136.5 112.5 all-reduce.2
  260.5 45.5 reduce-scatter.4
  308.9 30.4 all-gather.4
  350.1 112.5 all-reduce.4
where the time goes:
time: 507 us
  waiting for transfers between devices  379 us (75%)
  matrix products  49.6 us (10%)
  blocking collectives  41.2 us (8%)
  other arithmetic  19.9 us (4%)
  between operations  14.2 us (3%)
    psum x2, waiting for transfers between devices, residual_of(): summed = lax.psum(recon_part, 'atom')  225 us
    reduce_scatter x2, waiting for transfers between devices, body(): lax.psum_scatter(encode_rows(jnp.int32(0), lax.axis_size('dp') * row_coun...  92.9 us
    all_gather x2, waiting for transfers between devices, body(): lax.all_gather(sparse_codes.astype(jnp.bfloat16), 'dp', axis=0, tiled=True)  61 us
    dot_general x5, matrix products, product(): jnp.dot(left.astype(jnp.float32), right, precision=lax.Precision.HIGHEST,...  49.6 us
    all_to_all x1, blocking collectives, body(): lax.all_to_all(activations, 'dp', split_axis=1, concat_axis=0, tiled=True)  30.7 us
    convert_element_type x1, other arithmetic, body(): (updated * lax.rsqrt(squares / D + epsilon)).astype(jnp.bfloat16)  12.1 us
    psum x1, blocking collectives, body(): squares = lax.psum(jnp.sum(updated * updated, axis=0), 'dp')  10.5 us
  transfers between devices with their start and end apart: 6, of which 6 were waited for; matrix products, arithmetic and copies ran while one was open for 0% of the time, Pallas kernels for 0%

commit v1 on v0

--- a/solution.py
+++ b/solution.py
@@ -9,6 +9,15 @@
 step_size = 2.0
 learn_rate = 1.0 / 16384.0
 epsilon = 1e-12
+
+
+def sum_by_hops(block, axis):
+    size = lax.axis_size(axis)
+    acc, far = (block, 1)
+    while far < size:
+        acc = acc + lax.ppermute(acc, axis, [(i, i ^ far) for i in range(size)])
+        far = 2 * far
+    return acc
 
 
 def shrink(values):
@@ -34,7 +43,7 @@
 
     def residual_of(coded_rows):
         recon_part = product(coded_rows, dict_wide.T)
-        summed = lax.psum(recon_part, "atom")
+        summed = sum_by_hops(recon_part, "atom")
         full_residual = inputs - summed
         rounded = full_residual.astype(jnp.bfloat16)
         own_residual = lax.dynamic_slice_in_dim(full_residual, offset, share_rows, 0)

time: 507 us -> 1030 us (2.03)
  waiting for transfers between devices: 379 us -> 893 us
  starting transfers between devices: 0.43 us -> 15 us
  other arithmetic: 19.9 us -> 31.1 us
  matrix products: 49.6 us -> 39 us
    ppermute x0 -> x10, waiting for transfers between devices: none -> 737 us  [sum_by_hops(): acc = acc + lax.ppermute(acc, axis, [(i, i ^ far) for i in range(size)])]
    psum x2 -> x0, waiting for transfers between devices: 225 us -> none  [residual_of(): summed = lax.psum(recon_part, 'atom')]
    ppermute x0 -> x10, starting transfers between devices: none -> 14.6 us  [sum_by_hops(): acc = acc + lax.ppermute(acc, axis, [(i, i ^ far) for i in range(size)])]
    dot_general x5, matrix products: 49.6 us -> 39 us  [product(): jnp.dot(left.astype(jnp.float32), right, precision=lax.Precision.HIGHEST,...]
  transfers between devices with their start and end apart: 6 -> 14, of which waited for: 6 -> 14; matrix products, arithmetic and copies ran while one was open for 0% -> 0% of each run, Pallas kernels for 0% -> 0%
where the time goes in v1:
time: 1030 us
  waiting for transfers between devices  893 us (87%)
  blocking collectives  39.3 us (4%)
  matrix products  39 us (4%)
  other arithmetic  31.1 us (3%)
  starting transfers between devices  15 us (1%)
  between operations  13.9 us (1%)
    ppermute x10, waiting for transfers between devices, sum_by_hops(): acc = acc + lax.ppermute(acc, axis, [(i, i ^ far) for i in range(size)])  737 us
    reduce_scatter x2, waiting for transfers between devices, body(): lax.psum_scatter(encode_rows(jnp.int32(0), lax.axis_size('dp') * row_coun...  93.9 us
    all_gather x2, waiting for transfers between devices, body(): lax.all_gather(sparse_codes.astype(jnp.bfloat16), 'dp', axis=0, tiled=True)  61.2 us
    dot_general x5, matrix products, product(): jnp.dot(left.astype(jnp.float32), right, precision=lax.Precision.HIGHEST,...  39 us
    all_to_all x1, blocking collectives, body(): lax.all_to_all(activations, 'dp', split_axis=1, concat_axis=0, tiled=True)  30.7 us
  transfers between devices with their start and end apart: 14, of which 14 were waited for; matrix products, arithmetic and copies ran while one was open for 0% of the time, Pallas kernels for 0%

profile of v1, /device:TPU:24, one launch (start us, length us, event | category | flops | bytes accessed | tf_op | source)
XLA Modules:
  0.0 1033.4 jit_solution(10804878712237008179)
XLA Ops:
  7.2 0.0 reduce-scatter.3.cloned.1.call-start
  7.2 0.0 copy-start
  7.2 1.9 copy.8
  9.1 30.7 %all_to_all.19 = bf16[128,4,2048]{2,0,1:T(8,128)(2,1)S(1)} all-to-all(bf16[128,4,2048]{2,0,1:T(8,128)(2,1)S(1)} %bitcast.20), channel_id=1, replica_groups=mesh['atom'=32,'dp'=4] {'dp'}, dimensions={1} | all-to-all | bytes 4194304 | tf_op jit(solution)/shard_map/all_to_all | solution.py:39
  39.8 0.0 copy-done
  39.8 6.0 fusion.7
  45.8 0.0 reduce-scatter.3.cloned.1.call-update
  45.8 0.0 all-gather.3.cloned.1.call-start
  45.9 47.2 %reduce-scatter.3.cloned.1.call-done = f32[128,2048]{1,0:T(8,128)} async-done(((f32[512,2048]{1,0:T(8,128)}), f32[128,2048]{1,0:T(8,128)}) %reduce-scatter.3.cloned.1.call-update) | async-done | bytes 1048592 | tf_op jit(solution)/shard_map/reduce_scatter | solution.py:63
  93.0 2.2 fusion.5
  95.2 0.0 all-gather.3.cloned.1.call-update
  95.2 0.0 reduce-scatter.5.cloned.1.call-start
  95.3 30.6 %all-gather.3.cloned.1.call-done = bf16[512,2048]{1,0:T(8,128)(2,1)} async-done(((bf16[128,2048]{1,0:T(8,128)(2,1)}), bf16[512,2048]{1,0:T(8,128)(2,1)}) %all-gather.3.cloned.1.call-update) | async-done | bytes 2097168 | tf_op jit(solution)/shard_map/all_gather | solution.py:70
  125.8 7.6 fusion.8
  133.5 0.1 collective-permute-start
  133.6 7.1 collective-permute-done
  140.7 0.8 add.51
  141.6 0.9 collective-permute-start.1
  142.5 91.8 %collective-permute-done.1 = f32[512,2048]{1,0:T(8,128)S(1)} collective-permute-done((f32[512,2048]{1,0:T(8,128)S(1)}, f32[512,2048]{1,0:T(8,128)S(1)}, u32[]{:S(2)}, u32[]{:S(2)}) %collective-permute-start.1) | collective-permute-done | bytes 4194336 | tf_op jit(solution)/shard_map/ppermute | solution.py:18
  234.2 0.8 add.52
  235.1 1.5 collective-permute-start.2
  236.6 91.8 %collective-permute-done.2 = f32[512,2048]{1,0:T(8,128)S(1)} collective-permute-done((f32[512,2048]{1,0:T(8,128)S(1)}, f32[512,2048]{1,0:T(8,128)S(1)}, u32[]{:S(2)}, u32[]{:S(2)}) %collective-permute-start.2) | collective-permute-done | bytes 4194336 | tf_op jit(solution)/shard_map/ppermute | solution.py:18
  328.4 0.0 slice-start
  328.4 1.1 add.53
  329.5 0.0 slice-start.1
  329.5 1.6 collective-permute-start.3
  331.2 89.3 %collective-permute-done.3 = f32[512,2048]{1,0:T(8,128)S(1)} collective-permute-done((f32[512,2048]{1,0:T(8,128)S(1)}, f32[512,2048]{1,0:T(8,128)S(1)}, u32[]{:S(2)}, u32[]{:S(2)}) %collective-permute-start.3) | collective-permute-done | bytes 4194336 | tf_op jit(solution)/shard_map/ppermute | solution.py:18
  420.5 1.1 add.54
  421.6 3.2 collective-permute-start.4
  424.8 88.4 %collective-permute-done.4 = f32[512,2048]{1,0:T(8,128)S(1)} collective-permute-done((f32[512,2048]{1,0:T(8,128)S(1)}, f32[512,2048]{1,0:T(8,128)S(1)}, u32[]{:S(2)}, u32[]{:S(2)}) %collective-permute-start.4) | collective-permute-done | bytes 4194336 | tf_op jit(solution)/shard_map/ppermute | solution.py:18
  513.2 0.0 slice-done
  513.2 0.0 slice-done.1
  513.2 6.3 fusion.1
  519.6 0.0 copy-start.1
  519.6 0.0 reduce-scatter.5.cloned.1.call-update
  519.6 0.2 all-gather.5.cloned.1.call-start
  519.8 46.8 %reduce-scatter.5.cloned.1.call-done = f32[128,2048]{1,0:T(8,128)} async-done(((f32[512,2048]{1,0:T(8,128)}), f32[128,2048]{1,0:T(8,128)}) %reduce-scatter.5.cloned.1.call-update) | async-done | bytes 1048592 | tf_op jit(solution)/shard_map/reduce_scatter | solution.py:63
  566.6 0.0 copy-done.1
  566.6 2.6 fusion.6
  569.2 0.0 all-gather.5.cloned.1.call-update
  569.2 30.7 %all-gather.5.cloned.1.call-done = bf16[512,2048]{1,0:T(8,128)(2,1)} async-done(((bf16[128,2048]{1,0:T(8,128)(2,1)}), bf16[512,2048]{1,0:T(8,128)(2,1)}) %all-gather.5.cloned.1.call-update) | async-done | bytes 2097168 | tf_op jit(solution)/shard_map/all_gather | solution.py:70
  599.9 7.6 fusion.9
  607.5 0.1 collective-permute-start.5
  607.6 7.1 collective-permute-done.5
  614.8 0.8 add.57
  615.6 0.9 collective-permute-start.6
  616.5 91.8 %collective-permute-done.6 = f32[512,2048]{1,0:T(8,128)S(1)} collective-permute-done((f32[512,2048]{1,0:T(8,128)S(1)}, f32[512,2048]{1,0:T(8,128)S(1)}, u32[]{:S(2)}, u32[]{:S(2)}) %collective-permute-start.6) | collective-permute-done | bytes 4194336 | tf_op jit(solution)/shard_map/ppermute | solution.py:18
  708.3 1.1 add.58
  709.4 1.5 collective-permute-start.7
  710.9 91.8 %collective-permute-done.7 = f32[512,2048]{1,0:T(8,128)S(1)} collective-permute-done((f32[512,2048]{1,0:T(8,128)S(1)}, f32[512,2048]{1,0:T(8,128)S(1)}, u32[]{:S(2)}, u32[]{:S(2)}) %collective-permute-start.7) | collective-permute-done | bytes 4194336 | tf_op jit(solution)/shard_map/ppermute | solution.py:18
  802.7 1.1 add.59
  803.8 1.6 collective-permute-start.8
  805.4 89.4 %collective-permute-done.8 = f32[512,2048]{1,0:T(8,128)S(1)} collective-permute-done((f32[512,2048]{1,0:T(8,128)S(1)}, f32[512,2048]{1,0:T(8,128)S(1)}, u32[]{:S(2)}, u32[]{:S(2)}) %collective-permute-start.8) | collective-permute-done | bytes 4194336 | tf_op jit(solution)/shard_map/ppermute | solution.py:18
  894.8 2.8 add.60
  897.6 3.1 collective-permute-start.9
  900.7 0.0 copy-start.2
  900.7 88.7 %collective-permute-done.9 = f32[512,2048]{1,0:T(8,128)} collective-permute-done((f32[512,2048]{1,0:T(8,128)}, f32[512,2048]{1,0:T(8,128)}, u32[]{:S(2)}, u32[]{:S(2)}) %collective-permute-start.9) | collective-permute-done | bytes 4194336 | tf_op jit(solution)/shard_map/ppermute | solution.py:18
  989.4 4.6 convert_subtract_fusion
  994.0 0.7 constant_dynamic-slice_fusion
  994.7 0.0 copy-done.2
  994.7 11.4 %multiply_reduce_fusion = (f32[2048]{0:T(1024)S(1)}, f32[2048,2048]{1,0:T(8,128)}) fusion(bf16[2048,2048]{1,0:T(8,128)(2,1)} %param.3, bf16[512,2048]{1,0:T(8,128)(2,1)S(1)} %copy-done.2, f32[512,2048]{1,0:T(8,128)S(1)} %convert_subtract_fusion), kind=kOutput, calls=%fused_computation.1 | convolution fusion | flops 4316985344 | bytes 31465472 | tf_op jit(solution)/shard_map/dot_general | solution.py:28
  1006.1 8.6 psum.7
  1014.7 12.1 %multiply_convert_fusion = bf16[2048,2048]{1,0:T(8,128)(2,1)} fusion(f32[2048,2048]{1,0:T(8,128)} %get-tuple-element.6, bf16[2048,2048]{1,0:T(8,128)(2,1)} %param.3, f32[2048]{0:T(1024)S(1)} %add_rsqrt_fusion), kind=kLoop, calls=%fused_computation | loop fusion | flops 20971520 | bytes 33562624 | tf_op jit(solution)/shard_map/convert_element_type | solution.py:75
  (2 shorter events, 0.0 us)
Async XLA Ops:
  7.2 85.9 %reduce-scatter.3.cloned.1.call-start = ((), (), s32[]{:S(2)}) async-start(), calls=%async_computation.3 | async-start | bytes 5242880 | tf_op jit(solution)/shard_map/reduce_scatter | solution.py:63
  7.2 32.6 %copy-start = (bf16[2048,2048]{1,0:T(8,128)(2,1)S(1)}, bf16[2048,2048]{1,0:T(8,128)(2,1)}, u32[]{:S(2)}) copy-start(bf16[2048,2048]{1,0:T(8,128)(2,1)} %param.3) | copy-start | bytes 25165828
  45.8 80.0 %all-gather.3.cloned.1.call-start = ((), (), s32[]{:S(2)}) async-start(), calls=%async_computation.4 | async-start | bytes 2621440 | tf_op jit(solution)/shard_map/all_gather | solution.py:70
  95.2 471.4 %reduce-scatter.5.cloned.1.call-start = ((), (), s32[]{:S(2)}) async-start(), calls=%async_computation.5 | async-start | bytes 5242880 | tf_op jit(solution)/shard_map/reduce_scatter | solution.py:63
  133.5 7.2 collective-permute-start
  141.6 92.7 %collective-permute-start.1 = (f32[512,2048]{1,0:T(8,128)S(1)}, f32[512,2048]{1,0:T(8,128)S(1)}, u32[]{:S(2)}, u32[]{:S(2)}) collective-permute-start(f32[512,2048]{1,0:T(8,128)S(1)} %add.51), channel_id=1, source_target_pairs={{0,8},{4,12},{8,0},{12,4},{16,24},{20,28},{24,16},{28,20},{32,40},... | collective-permute-start | bytes 12582920 | tf_op jit(solution)/shard_map/ppermute | solution.py:18
  235.1 93.3 %collective-permute-start.2 = (f32[512,2048]{1,0:T(8,128)S(1)}, f32[512,2048]{1,0:T(8,128)S(1)}, u32[]{:S(2)}, u32[]{:S(2)}) collective-permute-start(f32[512,2048]{1,0:T(8,128)S(1)} %add.52), channel_id=1, source_target_pairs={{0,16},{4,20},{8,24},{12,28},{16,0},{20,4},{24,8},{28,12},{32,48},... | collective-permute-start | bytes 12582920 | tf_op jit(solution)/shard_map/ppermute | solution.py:18
  328.4 184.8 %slice-start = ((s8[8388608]{0:T(1024)(128)(4,1)}), s8[4194304]{0:T(1024)(128)(4,1)S(1)}, s32[]{:S(2)}) async-start(s8[8388608]{0:T(1024)(128)(4,1)} %bitcast.16), calls=%async_computation.7 | async-start | bytes 8388608
  329.5 183.7 %slice-start.1 = ((s8[8388608]{0:T(1024)(128)(4,1)}), s8[4194304]{0:T(1024)(128)(4,1)S(1)}, s32[]{:S(2)}) async-start(s8[8388608]{0:T(1024)(128)(4,1)} %bitcast.16), calls=%async_computation.8 | async-start | bytes 8388608
  329.5 91.0 %collective-permute-start.3 = (f32[512,2048]{1,0:T(8,128)S(1)}, f32[512,2048]{1,0:T(8,128)S(1)}, u32[]{:S(2)}, u32[]{:S(2)}) collective-permute-start(f32[512,2048]{1,0:T(8,128)S(1)} %add.53), channel_id=1, source_target_pairs={{0,32},{4,36},{8,40},{12,44},{16,48},{20,52},{24,56},{28,60},{32,0... | collective-permute-start | bytes 12582920 | tf_op jit(solution)/shard_map/ppermute | solution.py:18
  421.6 91.6 %collective-permute-start.4 = (f32[512,2048]{1,0:T(8,128)S(1)}, f32[512,2048]{1,0:T(8,128)S(1)}, u32[]{:S(2)}, u32[]{:S(2)}) collective-permute-start(f32[512,2048]{1,0:T(8,128)S(1)} %add.54), channel_id=1, source_target_pairs={{0,64},{4,68},{8,72},{12,76},{16,80},{20,84},{24,88},{28,92},{32,9... | collective-permute-start | bytes 12582920 | tf_op jit(solution)/shard_map/ppermute | solution.py:18
  519.6 47.0 %copy-start.1 = (f32[128,2048]{1,0:T(8,128)S(1)}, f32[128,2048]{1,0:T(8,128)}, u32[]{:S(2)}) copy-start(f32[128,2048]{1,0:T(8,128)} %reduce-scatter.3.cloned.1.call-done) | copy-start | bytes 3145732
  519.6 80.3 %all-gather.5.cloned.1.call-start = ((), (), s32[]{:S(2)}) async-start(), calls=%async_computation.6 | async-start | bytes 2621440 | tf_op jit(solution)/shard_map/all_gather | solution.py:70
  607.5 7.2 collective-permute-start.5
  615.6 92.7 %collective-permute-start.6 = (f32[512,2048]{1,0:T(8,128)S(1)}, f32[512,2048]{1,0:T(8,128)S(1)}, u32[]{:S(2)}, u32[]{:S(2)}) collective-permute-start(f32[512,2048]{1,0:T(8,128)S(1)} %add.57), channel_id=1, source_target_pairs={{0,8},{4,12},{8,0},{12,4},{16,24},{20,28},{24,16},{28,20},{32,40},... | collective-permute-start | bytes 12582920 | tf_op jit(solution)/shard_map/ppermute | solution.py:18
  709.4 93.3 %collective-permute-start.7 = (f32[512,2048]{1,0:T(8,128)S(1)}, f32[512,2048]{1,0:T(8,128)S(1)}, u32[]{:S(2)}, u32[]{:S(2)}) collective-permute-start(f32[512,2048]{1,0:T(8,128)S(1)} %add.58), channel_id=1, source_target_pairs={{0,16},{4,20},{8,24},{12,28},{16,0},{20,4},{24,8},{28,12},{32,48},... | collective-permute-start | bytes 12582920 | tf_op jit(solution)/shard_map/ppermute | solution.py:18
  803.8 91.0 %collective-permute-start.8 = (f32[512,2048]{1,0:T(8,128)S(1)}, f32[512,2048]{1,0:T(8,128)S(1)}, u32[]{:S(2)}, u32[]{:S(2)}) collective-permute-start(f32[512,2048]{1,0:T(8,128)S(1)} %add.59), channel_id=1, source_target_pairs={{0,32},{4,36},{8,40},{12,44},{16,48},{20,52},{24,56},{28,60},{32,0... | collective-permute-start | bytes 12582920 | tf_op jit(solution)/shard_map/ppermute | solution.py:18
  897.6 91.9 %collective-permute-start.9 = (f32[512,2048]{1,0:T(8,128)}, f32[512,2048]{1,0:T(8,128)}, u32[]{:S(2)}, u32[]{:S(2)}) collective-permute-start(f32[512,2048]{1,0:T(8,128)} %add.60), channel_id=1, source_target_pairs={{0,64},{4,68},{8,72},{12,76},{16,80},{20,84},{24,88},{28,92},{32,9... | collective-permute-start | bytes 12582920 | tf_op jit(solution)/shard_map/ppermute | solution.py:18
  900.7 94.0 %copy-start.2 = (bf16[512,2048]{1,0:T(8,128)(2,1)S(1)}, bf16[512,2048]{1,0:T(8,128)(2,1)}, u32[]{:S(2)}) copy-start(bf16[512,2048]{1,0:T(8,128)(2,1)} %all-gather.5.cloned.1.call-done) | copy-start | bytes 6291460
Sparse Core Ops, SparseCore 0:
  45.9 47.0 reduce-scatter.2
  95.3 30.4 all-gather.2
  519.7 46.8 reduce-scatter.4
  569.4 30.4 all-gather.4
